TPU v7x, 32 devices: a whole 2x2x4 slice. The times are simulated.
32 devices in a mesh: ckpt: 4 (over x, core), wide: 8 (over z, y).
Axes of the slice: x: 2, y: 2, z: 4, core: 2. Of those that a mesh axis runs over, the one named last changes fastest.
Arguments:
- codes: bfloat16 [4, 8, 8192, 1024], P('ckpt', 'wide'), may hold values from -4 to 4
- scales: float32 [4, 8, 8192, 8], P('ckpt', 'wide'), may hold values from 0.5 to 5
- example_ids: int32 [8, 8192], P('wide'), may hold values from 0 to 8191, each once within a row
- targets: bfloat16 [1024, 4096], P('wide'), may hold values from -0.09375 to 0.09375
- owners: int32 [6], replicated, may hold values from 0 to 7, as said below
Outputs:
- scores: float32 [8, 8192, 768], P('wide', 'ckpt')
Inputs may be any that keep to these rules, and one draw needn't show every extreme that they name: `example_ids`: each row is a permutation of the 8192 examples of its group. Distinct owners; owner 0 and owner 8 - 1 are always among them.
All inputs are finite; a program needn't handle non-finite values.
Results may differ from a plain program's by a relative error of at most 0.0029.
Values may be sent and summed in bfloat16 or wider, within the bound.
A program may use at most 192 MiB of HBM per device.

v0:
```python
import jax
import jax.numpy as jnp
from jax import lax
from jax.sharding import PartitionSpec as P


def from_root(shard, axis, root):
    mine = lax.axis_index(axis) == root
    return lax.psum(jnp.where(mine, shard, jnp.zeros_like(shard)), axis)


def fetch(targets, owner, width):
    piece = lax.dynamic_slice_in_dim(targets, lax.axis_index("ckpt") * width, width, 1)
    got = from_root(piece, "wide", owner)
    return lax.all_gather(got, "ckpt", axis=1, tiled=True)


def per_device(codes, scales, example_ids, targets, owners):
    width = codes.shape[-1]
    block = width // scales.shape[-1]
    feats = (codes[0, 0].astype(jnp.float32) * jnp.repeat(scales[0, 0], block, axis=-1)).astype(
        jnp.bfloat16
    )
    ordered = jnp.take(feats, example_ids[0], axis=0)
    rounds = owners.shape[0]
    contract = (((1,), (1,)), ((), ()))
    resident = lax.all_to_all(ordered, "ckpt", split_axis=0, concat_axis=1, tiled=True)
    columns = []
    for step in range(rounds):
        chosen = fetch(targets, owners[step], width)
        columns.append(
            lax.dot_general(resident, chosen, contract, preferred_element_type=jnp.float32)
        )
    result = jnp.concatenate(columns, axis=1)
    scale_factor = 1.0 / lax.axis_size("ckpt")
    return (result * scale_factor)[None]


def solution(mesh):
    return jax.shard_map(
        per_device,
        mesh=mesh,
        in_specs=(
            P("ckpt", "wide", None, None),
            P("ckpt", "wide", None, None),
            P("wide", None),
            P("wide", None),
            P(),
        ),
        out_specs=P("wide", "ckpt", None),
        check_vma=False,
    )
```

profile of v0, /device:TPU:28, one launch (start us, length us, event | category | flops | bytes accessed | tf_op | source)
XLA Modules:
  0.0 416.7 jit_solution(499906623515090295)
XLA Ops:
  6.5 3.5 copy.8
  10.1 0.8 compare_select_fusion
  10.9 10.3 %broadcast_in_dim.15 = f32[8192,8,128]{2,1,0:T(8,128)S(1)} broadcast(f32[8192,8]{1,0:T(8,128)} %copy.8), dimensions={0,1} | broadcast | bytes 33816576 | tf_op jit(solution)/shard_map/broadcast_in_dim | solution.py:21
  21.2 18.0 %fusion = bf16[8192,1024]{1,0:T(8,128)(2,1)} fusion(f32[1024,8,8,128]{3,2,1,0:T(8,128)S(1)} %bitcast.58, bf16[1,1,8192,1024]{3,2,1,0:T(8,128)(2,1)} %param.5), kind=kLoop, calls=%fused_computation.2 | loop fusion | flops 25165824 | bytes 67108864 | tf_op jit(solution)/shard_map/convert_element_type | solution.py:21
  39.1 48.4 %gather_fusion = bf16[8192,1024]{1,0:T(8,128)(2,1)} fusion(bf16[8192,1024]{1,0:T(8,128)(2,1)} %fusion, s32[8192]{0:T(1024)S(1)} %broadcast_clamp_fusion), kind=kCustom, calls=%fused_computation | custom fusion | bytes 33587200 | tf_op jit(solution)/shard_map/jit(_take)/gather | solution.py:24
  87.6 21.9 %copy.9 = bf16[4,2048,1024]{1,2,0:T(8,128)(2,1)} copy(bf16[4,2048,1024]{2,1,0:T(8,128)(2,1)} %bitcast.59) | data formatting | bytes 33554432 | tf_op jit(solution)/shard_map/jit(_take)/gather | solution.py:24
  109.5 0.5 broadcast.55
  110.0 0.7 reduce.3
  110.8 14.2 %broadcast_select_fusion = bf16[4,2048,1024]{1,2,0:T(8,128)(2,1)} fusion(bf16[4,2048,1024]{1,2,0:T(8,128)(2,1)} %copy.9, pred[4,2048]{1,0:T(4,128)(4,1)S(1)} %compare_and_fusion), kind=kLoop, calls=%fused_computation.3 | loop fusion | flops 8388608 | bytes 33562624 | tf_op jit(solution)/shard_map/jit(_take)/select_n | solution.py:24
  125.0 7.1 %all-to-all-start = ((bf16[4,2048,1024]{1,2,0:T(8,128)(2,1)}), bf16[4,2048,1024]{1,2,0:T(8,128)(2,1)}, u32[]{:S(2)}, u32[]{:S(2)}) async-start(bf16[4,2048,1024]{1,2,0:T(8,128)(2,1)} %broadcast_select_fusion), calls=%async_computation | async-start | bytes 33554432 | tf_op jit(solution)/shard_map/all_to_all | solution.py:27
  132.1 0.0 all-reduce.3.cloned.1.call-start
  132.1 0.7 fusion.7
  136.6 2.2 broadcast_select_fusion.1
  138.8 0.0 all-gather.7.cloned.1.call-start
  138.8 89.4 %all-reduce.3.cloned.1.call-done = (bf16[128,1024]{1,0:T(8,128)(2,1)}, bf16[128,1024]{1,0:T(8,128)(2,1)}, bf16[128,1024]{1,0:T(8,128)(2,1)}, bf16[128,1024]{1,0:...) async-done(((bf16[128,1024]{1,0:T(8,128)(2,1)}, bf16[128,1024]{1,0:T(8,128)(2,1)}, bf16[128,1024]{1,0:T(8,128)(2,1)}, bf16[128,1024]{1,0:T(8,128)(2,1)}, ...) | async-done | bytes 1572880 | tf_op jit(solution)/shard_map/psum | solution.py:9
  228.3 0.0 all-gather.9.cloned.1.call-start
  228.3 0.7 all-gather.9.cloned.1.call-update
  229.0 0.5 all-gather.11.cloned.1.call-update
  229.6 0.5 all-gather.13.cloned.1.call-update
  230.2 0.5 all-gather.15.cloned.1.call-update
  230.7 0.2 all-gather.17.cloned.1.call-start
  231.0 0.5 all-gather.17.cloned.1.call-update
  231.5 21.7 %all-gather.7.cloned.1.call-done = bf16[128,4096]{1,0:T(8,128)(2,1)} async-done(((bf16[128,1024]{1,0:T(8,128)(2,1)}), bf16[128,4096]{1,0:T(8,128)(2,1)}) %all-gather.7.cloned.1.call-update) | async-done | bytes 1048592 | tf_op jit(solution)/shard_map/all_gather | solution.py:15
  253.2 86.4 %all-to-all-done = bf16[4,2048,1024]{1,2,0:T(8,128)(2,1)} async-done(((bf16[4,2048,1024]{1,2,0:T(8,128)(2,1)}), bf16[4,2048,1024]{1,2,0:T(8,128)(2,1)}, u32[]{:S(2)}, u32[]{:S(2)}) %all-to-all-start) | async-done | bytes 16777248 | tf_op jit(solution)/shard_map/all_to_all | solution.py:27
  339.6 9.5 %fusion.6 = f32[1,2048,768]{1,2,0:T(8,128)} fusion(bf16[128,4096]{1,0:T(8,128)(2,1)} %all-gather.7.cloned.1.call-done, bf16[2048,4096]{0,1:T(8,128)(2,1)} %bitcast.6), kind=kOutput, calls=%fused_computation.16 | convolution fusion | flops 2147483648 | bytes 18874368 | tf_op jit(solution)/shard_map/dot_general | solution.py:32
  349.0 9.8 %fusion.5 = f32[1,2048,768]{1,2,0:T(8,128)} fusion(f32[1,2048,768]{1,2,0:T(8,128)} %fusion.6, bf16[128,4096]{1,0:T(8,128)(2,1)} %all-gather.9.cloned.1.call-done, bf16[2048,4096]{0,1:T(8,128)(2,1)} %bitcast.6), kind=kOutput, calls=%fused_computation.14 | convolution fusion | flops 2147483648 | bytes 18874368 | tf_op jit(solution)/shard_map/dot_general | solution.py:32
  358.8 9.5 %fusion.4 = f32[1,2048,768]{1,2,0:T(8,128)} fusion(f32[1,2048,768]{1,2,0:T(8,128)} %fusion.5, bf16[128,4096]{1,0:T(8,128)(2,1)} %all-gather.11.cloned.1.call-done, bf16[2048,4096]{0,1:T(8,128)(2,1)} %bitcast.6), kind=kOutput, calls=%fused_computation.12 | convolution fusion | flops 2147483648 | bytes 18874368 | tf_op jit(solution)/shard_map/dot_general | solution.py:32
  368.3 9.4 %fusion.3 = f32[1,2048,768]{1,2,0:T(8,128)} fusion(f32[1,2048,768]{1,2,0:T(8,128)} %fusion.4, bf16[128,4096]{1,0:T(8,128)(2,1)} %all-gather.13.cloned.1.call-done, bf16[2048,4096]{0,1:T(8,128)(2,1)} %bitcast.6), kind=kOutput, calls=%fused_computation.10 | convolution fusion | flops 2147483648 | bytes 18874368 | tf_op jit(solution)/shard_map/dot_general | solution.py:32
  377.7 9.4 %fusion.2 = f32[1,2048,768]{1,2,0:T(8,128)} fusion(f32[1,2048,768]{1,2,0:T(8,128)} %fusion.3, bf16[128,4096]{1,0:T(8,128)(2,1)} %all-gather.15.cloned.1.call-done, bf16[2048,4096]{0,1:T(8,128)(2,1)} %bitcast.6), kind=kOutput, calls=%fused_computation.8 | convolution fusion | flops 2147483648 | bytes 18874368 | tf_op jit(solution)/shard_map/dot_general | solution.py:32
  387.1 9.7 %fusion.1 = f32[1,2048,768]{1,2,0:T(8,128)} fusion(f32[1,2048,768]{1,2,0:T(8,128)} %fusion.2, bf16[128,4096]{1,0:T(8,128)(2,1)} %all-gather.17.cloned.1.call-done, bf16[2048,4096]{0,1:T(8,128)(2,1)} %bitcast.6), kind=kOutput, calls=%fused_computation.6 | convolution fusion | flops 2147483648 | bytes 18874368 | tf_op jit(solution)/shard_map/dot_general | solution.py:32
  396.8 6.6 %broadcast_multiply_fusion = f32[1,2048,768]{1,2,0:T(8,128)} fusion(f32[1,2048,768]{1,2,0:T(8,128)} %fusion.1), kind=kLoop, calls=%fused_computation.4 | loop fusion | flops 1572864 | bytes 12582912 | tf_op jit(solution)/shard_map/mul | solution.py:36
  403.3 6.6 %copy.10 = f32[1,2048,768]{2,1,0:T(8,128)} copy(f32[1,2048,768]{1,2,0:T(8,128)} %broadcast_multiply_fusion) | data formatting | bytes 12582912 | tf_op jit(solution)/shard_map/mul | solution.py:36
  (17 shorter events, 0.2 us)
Async XLA Ops:
  87.6 22.4 %copy-start = (s32[1,8192]{1,0:T(1,128)S(1)}, s32[1,8192]{1,0:T(1,128)}, u32[]{:S(2)}) copy-start(s32[1,8192]{1,0:T(1,128)} %param.7) | copy-start | bytes 98308
  125.0 7.2 %copy-start.1 = (s32[6]{0:T(128)S(1)}, s32[6]{0:T(128)}, u32[]{:S(2)}) copy-start(s32[6]{0:T(128)} %param.9) | copy-start | bytes 76
  125.0 214.6 %all-to-all-start = ((bf16[4,2048,1024]{1,2,0:T(8,128)(2,1)}), bf16[4,2048,1024]{1,2,0:T(8,128)(2,1)}, u32[]{:S(2)}, u32[]{:S(2)}) async-start(bf16[4,2048,1024]{1,2,0:T(8,128)(2,1)} %broadcast_select_fusion), calls=%async_computation | async-start | bytes 33554432 | tf_op jit(solution)/shard_map/all_to_all | solution.py:27
  132.1 96.2 %all-reduce.3.cloned.1.call-start = ((), (), s32[]{:S(2)}) async-start(), calls=%async_computation.7 | async-start | bytes 3145728 | tf_op jit(solution)/shard_map/psum | solution.py:9
  138.8 114.4 %all-gather.7.cloned.1.call-start = ((), (), s32[]{:S(2)}) async-start(), calls=%async_computation.1 | async-start | bytes 1310720 | tf_op jit(solution)/shard_map/all_gather | solution.py:15
  228.3 120.8 %all-gather.9.cloned.1.call-start = ((), (), s32[]{:S(2)}) async-start(), calls=%async_computation.2 | async-start | bytes 1310720 | tf_op jit(solution)/shard_map/all_gather | solution.py:15
  229.0 129.8 %all-gather.11.cloned.1.call-start = ((), (), s32[]{:S(2)}) async-start(), calls=%async_computation.3 | async-start | bytes 1310720 | tf_op jit(solution)/shard_map/all_gather | solution.py:15
  229.6 138.7 %all-gather.13.cloned.1.call-start = ((), (), s32[]{:S(2)}) async-start(), calls=%async_computation.4 | async-start | bytes 1310720 | tf_op jit(solution)/shard_map/all_gather | solution.py:15
  230.2 147.5 %all-gather.15.cloned.1.call-start = ((), (), s32[]{:S(2)}) async-start(), calls=%async_computation.5 | async-start | bytes 1310720 | tf_op jit(solution)/shard_map/all_gather | solution.py:15
  230.7 156.4 %all-gather.17.cloned.1.call-start = ((), (), s32[]{:S(2)}) async-start(), calls=%async_computation.6 | async-start | bytes 1310720 | tf_op jit(solution)/shard_map/all_gather | solution.py:15
Sparse Core Ops, SparseCore 0:
  138.9 89.2 all-reduce.2
  229.8 23.3 all-gather.6
  254.8 22.4 all-gather.8
  278.6 22.4 all-gather.10
  302.5 22.3 all-gather.12
  326.3 18.1 all-gather.14
  346.1 16.6 all-gather.16
where the time goes:
time: 418 us; the launch traced here: 417 us
  waiting for transfers between devices  200 us (48%)
  local copies, waits for them, and re-layouts  91.9 us (22%)
  matrix products  57.2 us (14%)
  other arithmetic  42.4 us (10%)
  between operations  17.3 us (4%)
  starting transfers between devices  7.55 us (2%)
    psum x1, waiting for transfers between devices, from_root(): return lax.psum(jnp.where(mine, shard, jnp.zeros_like(shard)), axis)  89.4 us
    all_to_all x1, waiting for transfers between devices, per_device(): lax.all_to_all(ordered, 'ckpt', split_axis=0, concat_axis=1, tiled=True)  86.4 us
    gather x2, local copies, waits for them, and re-layouts, per_device(): ordered = jnp.take(feats, example_ids[0], axis=0)  70.4 us
    dot_general x6, matrix products, per_device(): lax.dot_general(resident, chosen, contract, preferred_element_type=jnp.fl...  57.2 us
    all_gather x6, waiting for transfers between devices, fetch(): return lax.all_gather(got, 'ckpt', axis=1, tiled=True)  21.7 us
    convert_element_type x1, other arithmetic, per_device(): (codes[0, 0].astype(jnp.float32) * jnp.repeat(scales[0, 0], block, axis=-...  18 us
    select_n x2, other arithmetic, per_device(): ordered = jnp.take(feats, example_ids[0], axis=0)  15 us
    broadcast_in_dim x1, local copies, waits for them, and re-layouts, per_device(): jnp.repeat(scales[0, 0], block, axis=-1)  10.3 us
  transfers between devices with their start and end apart: 8, of which 3 were waited for; matrix products, arithmetic and copies ran while one was open for 12% of the time, Pallas kernels for 0%

commit v1 on v0

--- a/solution.py
+++ b/solution.py
@@ -2,6 +2,22 @@
 import jax.numpy as jnp
 from jax import lax
 from jax.sharding import PartitionSpec as P
+
+
+def swapped_with_each(x, axis, split, join):
+    ways, here = (lax.axis_size(axis), lax.axis_index(axis))
+    width = x.shape[split] // ways
+    lengths = list(x.shape)
+    lengths[split] = width
+    height = lengths[join]
+    lengths[join] = height * ways
+    full = jnp.zeros(lengths, x.dtype)
+    for mask in range(ways):
+        part = lax.dynamic_slice_in_dim(x, (here ^ mask) * width, width, axis=split)
+        if mask:
+            part = lax.ppermute(part, axis, [(d, d ^ mask) for d in range(ways)])
+        full = lax.dynamic_update_slice_in_dim(full, part, (here ^ mask) * height, axis=join)
+    return full
 
 
 def from_root(shard, axis, root):
@@ -24,7 +40,7 @@
     ordered = jnp.take(feats, example_ids[0], axis=0)
     rounds = owners.shape[0]
     contract = (((1,), (1,)), ((), ()))
-    resident = lax.all_to_all(ordered, "ckpt", split_axis=0, concat_axis=1, tiled=True)
+    resident = swapped_with_each(ordered, "ckpt", 0, 1)
     columns = []
     for step in range(rounds):
         chosen = fetch(targets, owners[step], width)

time: 418 us -> 489 us (1.17)
  waiting for transfers between devices: 200 us -> 245 us
  matrix products: 57.2 us -> 75.9 us
  local copies, waits for them, and re-layouts: 91.9 us -> 102 us
  starting transfers between devices: 7.55 us -> 2.29 us
    ppermute x0 -> x3, waiting for transfers between devices: none -> 187 us  [swapped_with_each(): part = lax.ppermute(part, axis, [(d, d ^ mask) for d in range(ways)])]
    all_to_all x1 -> x0, waiting for transfers between devices: 86.4 us -> none  [per_device(): lax.all_to_all(ordered, 'ckpt', split_axis=0, concat_axis=1, tiled=True)]
    psum x1, waiting for transfers between devices: 89.4 us -> 57.1 us  [from_root(): return lax.psum(jnp.where(mine, shard, jnp.zeros_like(shard)), axis)]
    all_gather x6, waiting for transfers between devices: 21.7 us -> 0.01 us  [fetch(): return lax.all_gather(got, 'ckpt', axis=1, tiled=True)]
    gather x2 -> x1, local copies, waits for them, and re-layouts: 70.4 us -> 48.7 us  [per_device(): ordered = jnp.take(feats, example_ids[0], axis=0)]
    dot_general x6, matrix products: 57.2 us -> 75.9 us  [per_device(): lax.dot_general(resident, chosen, contract, preferred_element_type=jnp.fl...]
    dynamic_update_slice x0 -> x3, local copies, waits for them, and re-layouts: none -> 13.9 us  [swapped_with_each(): lax.dynamic_update_slice_in_dim(full, part, (here ^ mask) * height, axis=...]
    broadcast_in_dim x0 -> x1, local copies, waits for them, and re-layouts: none -> 8.37 us  [swapped_with_each(): full = jnp.zeros(lengths, x.dtype)]
  transfers between devices with their start and end apart: 8 -> 10, of which waited for: 3 -> 4; matrix products, arithmetic and copies ran while one was open for 12% -> 39% of each run, Pallas kernels for 0% -> 0%
where the time goes in v1:
time: 489 us; the launch traced here: 484 us
  waiting for transfers between devices  245 us (50%)
  local copies, waits for them, and re-layouts  102 us (21%)
  matrix products  75.9 us (16%)
  other arithmetic  41.1 us (8%)
  between operations  17.4 us (4%)
    ppermute x3, waiting for transfers between devices, swapped_with_each(): part = lax.ppermute(part, axis, [(d, d ^ mask) for d in range(ways)])  187 us
    dot_general x6, matrix products, per_device(): lax.dot_general(resident, chosen, contract, preferred_element_type=jnp.fl...  75.9 us
    psum x1, waiting for transfers between devices, from_root(): return lax.psum(jnp.where(mine, shard, jnp.zeros_like(shard)), axis)  57.1 us
    gather x1, local copies, waits for them, and re-layouts, per_device(): ordered = jnp.take(feats, example_ids[0], axis=0)  48.7 us
    convert_element_type x1, other arithmetic, per_device(): (codes[0, 0].astype(jnp.float32) * jnp.repeat(scales[0, 0], block, axis=-...  18 us
    select_n x2, other arithmetic, per_device(): ordered = jnp.take(feats, example_ids[0], axis=0)  14.3 us
    dynamic_update_slice x3, local copies, waits for them, and re-layouts, swapped_with_each(): lax.dynamic_update_slice_in_dim(full, part, (here ^ mask) * height, axis=...  13.9 us
    broadcast_in_dim x1, local copies, waits for them, and re-layouts, per_device(): jnp.repeat(scales[0, 0], block, axis=-1)  10.3 us
  transfers between devices with their start and end apart: 10, of which 4 were waited for; matrix products, arithmetic and copies ran while one was open for 39% of the time, Pallas kernels for 0%

profile of v1, /device:TPU:28, one launch (start us, length us, event | category | flops | bytes accessed | tf_op | source)
XLA Modules:
  0.0 484.3 jit_solution(1727324952885623996)
XLA Ops:
  6.5 1.6 fusion.7
  11.9 2.2 broadcast_select_fusion.1
  14.2 0.0 all-gather.7.cloned.1.call-start
  14.2 3.5 copy.8
  17.7 10.3 %broadcast_in_dim.19 = f32[8192,8,128]{2,1,0:T(8,128)S(1)} broadcast(f32[8192,8]{1,0:T(8,128)} %copy.8), dimensions={0,1} | broadcast | bytes 33816576 | tf_op jit(solution)/shard_map/broadcast_in_dim | solution.py:37
  28.0 18.0 %fusion = bf16[8192,1024]{1,0:T(8,128)(2,1)} fusion(f32[1024,8,8,128]{3,2,1,0:T(8,128)S(1)} %bitcast.55, bf16[1,1,8192,1024]{3,2,1,0:T(8,128)(2,1)} %param.5), kind=kLoop, calls=%fused_computation.2 | loop fusion | flops 25165824 | bytes 67108864 | tf_op jit(solution)/shard_map/convert_element_type | solution.py:37
  46.1 57.1 %all-reduce.3.cloned.1.call-done = (bf16[128,1024]{1,0:T(8,128)(2,1)}, bf16[128,1024]{1,0:T(8,128)(2,1)}, bf16[128,1024]{1,0:T(8,128)(2,1)}, bf16[128,1024]{1,0:...) async-done(((bf16[128,1024]{1,0:T(8,128)(2,1)}, bf16[128,1024]{1,0:T(8,128)(2,1)}, bf16[128,1024]{1,0:T(8,128)(2,1)}, bf16[128,1024]{1,0:T(8,128)(2,1)}, ...) | async-done | bytes 1572880 | tf_op jit(solution)/shard_map/psum | solution.py:25
  103.3 48.7 %gather_fusion = bf16[8192,1024]{1,0:T(8,128)(2,1)} fusion(bf16[8192,1024]{1,0:T(8,128)(2,1)} %fusion, s32[8192]{0:T(1024)S(1)} %broadcast_clamp_fusion), kind=kCustom, calls=%fused_computation | custom fusion | bytes 33587200 | tf_op jit(solution)/shard_map/jit(_take)/gather | solution.py:40
  152.1 0.0 all-gather.11.cloned.1.call-start
  152.1 14.3 %broadcast_select_fusion = bf16[8192,1024]{1,0:T(8,128)(2,1)} fusion(bf16[8192,1024]{1,0:T(8,128)(2,1)} %gather_fusion, pred[8192]{0:T(1024)(128)(4,1)S(1)} %compare_and_fusion), kind=kLoop, calls=%fused_computation.3 | loop fusion | flops 8388608 | bytes 33562624 | tf_op jit(solution)/shard_map/jit(_take)/select_n | solution.py:40
  166.5 8.4 %broadcast_in_dim.17 = bf16[2048,4096]{1,0:T(8,128)(2,1)} broadcast(bf16[]{:T(256)} %constant.14.clone.1), dimensions={} | broadcast | bytes 16777218 | tf_op jit(solution)/shard_map/broadcast_in_dim | solution.py:14
  174.8 3.1 copy-done
  178.0 6.1 %constant_dynamic-slice_fusion = (bf16[2048,1024]{1,0:T(8,128)(2,1)}, bf16[2048,1024]{1,0:T(8,128)(2,1)}, bf16[2048,1024]{1,0:T(8,128)(2,1)}, bf16[2048,4096]{1,0:T(8,128)(2,1)}) fusion(bf16[8192,1024]{1,0:T(8,128)(2,1)S(1)} %copy-done, s32[]{:T(128)S(6)} %select_n.97, s32[]{:T(128)S(6)} %select_n.95, s32[]{:T(128)S(6)} %select_n.93, ...), kind=kLoop, calls=%fused_computation.29 | loop fusion | bytes 33554452 | tf_op jit(solution)/shard_map/dynamic_slice | solution.py:16
  184.1 1.5 collective-permute-start.1
  185.6 0.3 collective-permute-start.2
  186.0 0.5 all-gather.15.cloned.1.call-update
  186.5 0.2 all-gather.17.cloned.1.call-start
  186.8 0.5 all-gather.17.cloned.1.call-update
  187.3 4.4 collective-permute-done
  191.7 4.6 constant_dynamic-update-slice_fusion.2
  196.3 98.4 %collective-permute-done.1 = bf16[2048,1024]{1,0:T(8,128)(2,1)} collective-permute-done((bf16[2048,1024]{1,0:T(8,128)(2,1)}, bf16[2048,1024]{1,0:T(8,128)(2,1)}, u32[]{:S(2)}, u32[]{:S(2)}) %collective-permute-start.1) | collective-permute-done | bytes 4194336 | tf_op jit(solution)/shard_map/ppermute | solution.py:18
  294.7 4.6 constant_dynamic-update-slice_fusion.1
  299.3 84.4 %collective-permute-done.2 = bf16[2048,1024]{1,0:T(8,128)(2,1)} collective-permute-done((bf16[2048,1024]{1,0:T(8,128)(2,1)}, bf16[2048,1024]{1,0:T(8,128)(2,1)}, u32[]{:S(2)}, u32[]{:S(2)}) %collective-permute-start.2) | collective-permute-done | bytes 4194336 | tf_op jit(solution)/shard_map/ppermute | solution.py:18
  383.7 4.7 constant_dynamic-update-slice_fusion
  388.4 12.6 %fusion.6 = f32[1,2048,768]{1,2,0:T(8,128)} fusion(bf16[2048,4096]{1,0:T(8,128)(2,1)} %constant_dynamic-update-slice_fusion, bf16[128,4096]{1,0:T(8,128)(2,1)} %all-gather.7.cloned.1.call-done), kind=kOutput, calls=%fused_computation.17 | convolution fusion | flops 2147483648 | bytes 18874368 | tf_op jit(solution)/shard_map/dot_general | solution.py:48
  401.0 12.6 %fusion.5 = f32[1,2048,768]{1,2,0:T(8,128)} fusion(f32[1,2048,768]{1,2,0:T(8,128)} %fusion.6, bf16[2048,4096]{1,0:T(8,128)(2,1)} %constant_dynamic-update-slice_fusion, bf16[128,4096]{1,0:T(8,128)(2,1)} %all-gather.9.cloned.1.call-done), kind=kOutput, calls=%fused_computation.15 | convolution fusion | flops 2147483648 | bytes 18874368 | tf_op jit(solution)/shard_map/dot_general | solution.py:48
  413.6 12.8 %fusion.4 = f32[1,2048,768]{1,2,0:T(8,128)} fusion(f32[1,2048,768]{1,2,0:T(8,128)} %fusion.5, bf16[2048,4096]{1,0:T(8,128)(2,1)} %constant_dynamic-update-slice_fusion, bf16[128,4096]{1,0:T(8,128)(2,1)} %all-gather.11.cloned.1.call-done), kind=kOutput, calls=%fused_computation.13 | convolution fusion | flops 2147483648 | bytes 18874368 | tf_op jit(solution)/shard_map/dot_general | solution.py:48
  426.4 12.6 %fusion.3 = f32[1,2048,768]{1,2,0:T(8,128)} fusion(f32[1,2048,768]{1,2,0:T(8,128)} %fusion.4, bf16[2048,4096]{1,0:T(8,128)(2,1)} %constant_dynamic-update-slice_fusion, bf16[128,4096]{1,0:T(8,128)(2,1)} %all-gather.13.cloned.1.call-done), kind=kOutput, calls=%fused_computation.11 | convolution fusion | flops 2147483648 | bytes 18874368 | tf_op jit(solution)/shard_map/dot_general | solution.py:48
  439.0 12.6 %fusion.2 = f32[1,2048,768]{1,2,0:T(8,128)} fusion(f32[1,2048,768]{1,2,0:T(8,128)} %fusion.3, bf16[2048,4096]{1,0:T(8,128)(2,1)} %constant_dynamic-update-slice_fusion, bf16[128,4096]{1,0:T(8,128)(2,1)} %all-gather.15.cloned.1.call-done), kind=kOutput, calls=%fused_computation.9 | convolution fusion | flops 2147483648 | bytes 18874368 | tf_op jit(solution)/shard_map/dot_general | solution.py:48
  451.7 12.6 %fusion.1 = f32[1,2048,768]{1,2,0:T(8,128)} fusion(f32[1,2048,768]{1,2,0:T(8,128)} %fusion.2, bf16[2048,4096]{1,0:T(8,128)(2,1)} %constant_dynamic-update-slice_fusion, bf16[128,4096]{1,0:T(8,128)(2,1)} %all-gather.17.cloned.1.call-done), kind=kOutput, calls=%fused_computation.7 | convolution fusion | flops 2147483648 | bytes 18874368 | tf_op jit(solution)/shard_map/dot_general | solution.py:48
  464.3 6.6 %broadcast_multiply_fusion = f32[1,2048,768]{1,2,0:T(8,128)} fusion(f32[1,2048,768]{1,2,0:T(8,128)} %fusion.1), kind=kLoop, calls=%fused_computation.5 | loop fusion | flops 1572864 | bytes 12582912 | tf_op jit(solution)/shard_map/mul | solution.py:52
  470.8 6.6 %copy.9 = f32[1,2048,768]{2,1,0:T(8,128)} copy(f32[1,2048,768]{1,2,0:T(8,128)} %broadcast_multiply_fusion) | data formatting | bytes 12582912 | tf_op jit(solution)/shard_map/mul | solution.py:52
  (22 shorter events, 0.3 us)
Async XLA Ops:
  6.5 96.7 %all-reduce.3.cloned.1.call-start = ((), (), s32[]{:S(2)}) async-start(), calls=%async_computation.6 | async-start | bytes 3145728 | tf_op jit(solution)/shard_map/psum | solution.py:25
  14.2 374.2 %all-gather.7.cloned.1.call-start = ((), (), s32[]{:S(2)}) async-start(), calls=%async_computation | async-start | bytes 1310720 | tf_op jit(solution)/shard_map/all_gather | solution.py:31
  28.0 75.2 %copy-start.1 = (s32[1,8192]{1,0:T(1,128)S(1)}, s32[1,8192]{1,0:T(1,128)}, u32[]{:S(2)}) copy-start(s32[1,8192]{1,0:T(1,128)} %param.7) | copy-start | bytes 98308
  103.2 297.8 %all-gather.9.cloned.1.call-start = ((), (), s32[]{:S(2)}) async-start(), calls=%async_computation.1 | async-start | bytes 1310720 | tf_op jit(solution)/shard_map/all_gather | solution.py:31
  152.1 261.5 %all-gather.11.cloned.1.call-start = ((), (), s32[]{:S(2)}) async-start(), calls=%async_computation.2 | async-start | bytes 1310720 | tf_op jit(solution)/shard_map/all_gather | solution.py:31
  166.4 260.0 %all-gather.13.cloned.1.call-start = ((), (), s32[]{:S(2)}) async-start(), calls=%async_computation.3 | async-start | bytes 1310720 | tf_op jit(solution)/shard_map/all_gather | solution.py:31
  166.4 11.5 %copy-start = (bf16[8192,1024]{1,0:T(8,128)(2,1)S(1)}, bf16[8192,1024]{1,0:T(8,128)(2,1)}, u32[]{:S(2)}) copy-start(bf16[8192,1024]{1,0:T(8,128)(2,1)} %broadcast_select_fusion) | copy-start | bytes 50331652
  184.1 7.6 %collective-permute-start = (bf16[2048,1024]{1,0:T(8,128)(2,1)}, bf16[2048,1024]{1,0:T(8,128)(2,1)}, u32[]{:S(2)}, u32[]{:S(2)}) collective-permute-start(bf16[2048,1024]{1,0:T(8,128)(2,1)} %get-tuple-element.13), channel_id=1, source_target_pairs={{0,8},{8,0},{16,24},{24,16},{1,9},{9,1},{17,25},{25,17},{2,10},{10... | collective-permute-start | bytes 12582920 | tf_op jit(solution)/shard_map/ppermute | solution.py:18
  184.1 110.6 %collective-permute-start.1 = (bf16[2048,1024]{1,0:T(8,128)(2,1)}, bf16[2048,1024]{1,0:T(8,128)(2,1)}, u32[]{:S(2)}, u32[]{:S(2)}) collective-permute-start(bf16[2048,1024]{1,0:T(8,128)(2,1)} %get-tuple-element.12), channel_id=1, source_target_pairs={{0,16},{8,24},{16,0},{24,8},{1,17},{9,25},{17,1},{25,9},{2,18},{10... | collective-permute-start | bytes 12582920 | tf_op jit(solution)/shard_map/ppermute | solution.py:18
  185.6 198.0 %collective-permute-start.2 = (bf16[2048,1024]{1,0:T(8,128)(2,1)}, bf16[2048,1024]{1,0:T(8,128)(2,1)}, u32[]{:S(2)}, u32[]{:S(2)}) collective-permute-start(bf16[2048,1024]{1,0:T(8,128)(2,1)} %get-tuple-element.11), channel_id=1, source_target_pairs={{0,24},{8,16},{16,8},{24,0},{1,25},{9,17},{17,9},{25,1},{2,26},{10... | collective-permute-start | bytes 12582920 | tf_op jit(solution)/shard_map/ppermute | solution.py:18
  186.0 253.1 %all-gather.15.cloned.1.call-start = ((), (), s32[]{:S(2)}) async-start(), calls=%async_computation.4 | async-start | bytes 1310720 | tf_op jit(solution)/shard_map/all_gather | solution.py:31
  186.5 265.1 %all-gather.17.cloned.1.call-start = ((), (), s32[]{:S(2)}) async-start(), calls=%async_computation.5 | async-start | bytes 1310720 | tf_op jit(solution)/shard_map/all_gather | solution.py:31
Sparse Core Ops, SparseCore 0:
  14.3 88.8 all-reduce.2
  104.8 17.6 all-gather.6
  152.2 17.6 all-gather.8
  171.3 16.7 all-gather.10
  189.4 22.4 all-gather.12
  213.3 22.4 all-gather.14
  237.3 22.4 all-gather.16
